TPU v7x, 32 devices: a whole 2x2x4 slice. The times are simulated.
32 devices in a mesh: blk: 8 (over z, y), frames: 4 (over x, core).
Axes of the slice: x: 2, y: 2, z: 4, core: 2. Of those that a mesh axis runs over, the one named last changes fastest.
Arguments:
- coarse_query: bfloat16 [64, 16, 256], P('blk'), may hold values from -125 to 125
- coarse_feat: bfloat16 [16, 8160, 256], P('frames', 'blk'), may hold values from -61 to 61
- fine_query: bfloat16 [64, 128], P(('blk', 'frames')), may hold values from -175 to 175
- fine_tiles: bfloat16 [16, 512, 64, 128], P('frames', 'blk'), may hold values from -61 to 61
- track_pos: int32 [2, 16, 64], P(None, None, ('blk', 'frames')), may hold values from 0 to 959, as said below
- tile_list: int32 [16, 8, 4, 8], P('frames', 'blk'), may hold values from 0 to 63, as said below
- tile_valid: int32 [16, 8, 4, 8], P('frames', 'blk'), may hold values from 0 to 1, as said below
Outputs:
- coarse_pos: float32 [2, 16, 64], P(None, 'frames', 'blk')
- fine_offset: float32 [2, 16, 64], P(None, None, ('blk', 'frames'))
Inputs may be any that keep to these rules, and one draw needn't show every extreme that they name: `tile_list`: in each list the valid slots come first and name distinct tiles of the group's window; padded slots hold 63; in every frame and group some owner's list is full. `tile_valid`: each list has at least 4 valid slots. `track_pos`: rows lie below 544 and columns below 960.
All inputs are finite; a program needn't handle non-finite values.
Results may differ from a plain program's by a relative error of at most 0.0003.
Values may be sent and summed in bfloat16 or wider, within the bound.
No kernel may reach another device: no remote copies, remote signals or barrier semaphores. Data moves between devices by JAX's collectives and lax.ppermute only.
A program may use at most 192 MiB of HBM per device.

v0:
```python
import math
import jax
import jax.numpy as jnp
from jax import lax
from jax.sharding import PartitionSpec as P

GH = 68
GW = 120
TILE = 8
spread_cells = 32.0


def refine_frame(descriptors, tile_block, tile_ids, tile_live, track_row, track_col, base_cell):
    slot_count, cell_count, channels = tile_block.shape
    flat_tiles = tile_block.reshape(slot_count * cell_count, channels)
    scores = jnp.einsum(
        "nc,kc->nk", descriptors, flat_tiles, preferred_element_type=jnp.float32
    ) * (1.0 / math.sqrt(channels))
    global_cell = base_cell + tile_ids
    inner_cell = jnp.arange(cell_count, dtype=jnp.int32)
    cell_row = (global_cell // GW * TILE)[:, None] + (inner_cell // TILE)[None, :]
    cell_col = (global_cell % GW * TILE)[:, None] + (inner_cell % TILE)[None, :]
    cell_row = cell_row.reshape(-1).astype(jnp.float32)
    cell_col = cell_col.reshape(-1).astype(jnp.float32)
    distance = (cell_row[None, :] - track_row[:, None]) ** 2 + (
        cell_col[None, :] - track_col[:, None]
    ) ** 2
    scores = scores - distance * (0.5 / (spread_cells * spread_cells))
    live_cells = jnp.broadcast_to(tile_live[:, None] > 0, (slot_count, cell_count)).reshape(-1)
    scores = jnp.where(live_cells[None, :], scores, -1e30)
    highest = jnp.max(scores, axis=1, keepdims=True)
    weights = jnp.exp(scores - highest)
    totals = jnp.sum(weights, axis=1)
    mean_row = jnp.sum(weights * cell_row[None, :], axis=1) / totals
    mean_col = jnp.sum(weights * cell_col[None, :], axis=1) / totals
    return ((mean_row - track_row) / spread_cells, (mean_col - track_col) / spread_cells)


def coarse_finish(row_mean, col_mean):
    row_heads = jnp.mean(row_mean, axis=2)
    col_heads = jnp.mean(col_mean, axis=2)
    return jnp.stack(
        [(row_heads - (GH - 1) / 2.0) / (GH / 4.0), (col_heads - (GW - 1) / 2.0) / (GW / 4.0)]
    )


def body(coarse_query, coarse_feat, fine_query, fine_tiles, track_pos, tile_list, tile_valid):
    track_group, heads, channels = coarse_query.shape
    frames_here, region, _ = coarse_feat.shape
    scale = 1.0 / math.sqrt(channels)
    group_start = lax.axis_index("blk") * region
    local_cells = group_start + jnp.arange(region, dtype=jnp.int32)
    local_row = (local_cells // GW).astype(jnp.float32)
    local_col = (local_cells % GW).astype(jnp.float32)
    track_step = max(1, 2048 // heads)
    shard_piece = lax.all_gather(coarse_query, "blk", axis=0, tiled=True)
    length = shard_piece.shape[0]
    blocks = []
    for offset in range(0, length, track_step):
        query_rows = shard_piece[offset : offset + track_step].reshape(-1, channels)
        scores = (
            jnp.einsum("rc,fpc->frp", query_rows, coarse_feat, preferred_element_type=jnp.float32)
            * scale
        )
        block_max = jnp.max(scores, axis=2)
        weights = jnp.exp(scores - block_max[:, :, None])
        totals = jnp.sum(weights, axis=2)
        row_sums = jnp.sum(weights * local_row[None, None, :], axis=2)
        col_sums = jnp.sum(weights * local_col[None, None, :], axis=2)
        stacked = jnp.stack([block_max, totals, row_sums, col_sums])
        blocks.append(stacked.reshape(4, frames_here, -1, heads))
    stats = jnp.concatenate(blocks, axis=2)
    maxima_all, totals_all, rows_all, cols_all = (
        lax.all_to_all(stats[0][None], "blk", split_axis=2, concat_axis=0, tiled=True),
        lax.all_to_all(stats[1][None], "blk", split_axis=2, concat_axis=0, tiled=True),
        lax.all_to_all(stats[2][None], "blk", split_axis=2, concat_axis=0, tiled=True),
        lax.all_to_all(stats[3][None], "blk", split_axis=2, concat_axis=0, tiled=True),
    )
    overall = jnp.max(maxima_all, axis=0)
    retain = jnp.exp(maxima_all - overall[None])
    totals = jnp.sum(totals_all * retain, axis=0)
    row_mean = jnp.sum(rows_all * retain, axis=0) / totals
    col_mean = jnp.sum(cols_all * retain, axis=0) / totals
    coarse_pos = coarse_finish(row_mean, col_mean)
    list_ids = jnp.transpose(tile_list[:, 0], (1, 0, 2))
    list_live = jnp.transpose(tile_valid[:, 0], (1, 0, 2))
    picked = fine_tiles[jnp.arange(frames_here, dtype=jnp.int32)[None, :, None], list_ids]
    per_frame = jax.vmap(refine_frame, in_axes=(None, 0, 0, 0, 0, 0, None))
    got_tiles, got_ids, got_live = (
        lax.all_to_all(picked, "frames", split_axis=0, concat_axis=0, tiled=True),
        lax.all_to_all(list_ids, "frames", split_axis=0, concat_axis=0, tiled=True),
        lax.all_to_all(list_live, "frames", split_axis=0, concat_axis=0, tiled=True),
    )
    window = got_tiles.shape[0] * got_tiles.shape[1]
    got_tiles = got_tiles.reshape((window,) + got_tiles.shape[2:])
    got_ids = got_ids.reshape(window, -1)
    got_live = got_live.reshape(window, -1)
    places = track_pos.astype(jnp.float32)
    rows_out, cols_out = per_frame(
        fine_query, got_tiles, got_ids, got_live, places[0], places[1], group_start
    )
    fine_offset = jnp.stack([rows_out, cols_out])
    return (coarse_pos, fine_offset)


def solution(mesh):
    return jax.shard_map(
        body,
        mesh=mesh,
        in_specs=(
            P("blk", None, None),
            P("frames", "blk", None),
            P(("blk", "frames"), None),
            P("frames", "blk", None, None),
            P(None, None, ("blk", "frames")),
            P("frames", "blk", None, None),
            P("frames", "blk", None, None),
        ),
        out_specs=(P(None, "frames", "blk"), P(None, None, ("blk", "frames"))),
        check_vma=False,
    )
```

profile of v0, /device:TPU:0, one launch (start us, length us, event | category | flops | bytes accessed | tf_op | source)
XLA Modules:
  0.0 131.4 jit_solution(15096075007774949276)
XLA Ops:
  0.6 1.3 copy.64
  1.9 4.2 %all-to-all-start.6 = ((s32[4,4,8]{2,1,0:T(4,128)}), s32[4,4,8]{2,1,0:T(4,128)S(1)}, u32[]{:S(2)}, u32[]{:S(2)}) async-start(s32[4,4,8]{2,1,0:T(4,128)} %copy.64), calls=%async_computation.6 | async-start | bytes 16384 | tf_op jit(solution)/shard_map/all_to_all | solution.py:91
  6.2 0.7 fusion.13
  6.9 32.6 %all_gather.3 = bf16[64,16,256]{2,1,0:T(8,128)(2,1)S(1)} all-gather(bf16[8,16,256]{2,1,0:T(8,128)(2,1)} %param.7), channel_id=1, replica_groups=mesh['blk'=8,'frames'=4] {'blk'}, dimensions={0}, use_global_device_ids=true | all-gather | bytes 589824 | tf_op jit(solution)/shard_map/all_gather | solution.py:56
  39.5 4.0 %bitcast_reduce_fusion = (f32[4,1024]{1,0:T(4,128)S(1)}, f32[4,1020,1024]{2,1,0:T(8,128)S(1)}) fusion(bf16[1024,256,1]{1,0,2:T(8,128)(2,1)S(1)} %bitcast.96, bf16[4,1020,256]{2,0,1:T(4,128)(2,1)} %param.8), kind=kOutput, calls=%fused_computation.3 | convolution fusion | flops 2147446784 | bytes 19341312 | tf_op jit(solution)/shard_map/rc,fpc->frp/dot_general | solution.py:62
  43.5 5.9 %multiply_reduce_fusion.1 = (f32[4,1024]{1,0:T(4,128)S(1)}, f32[4,1024]{1,0:T(4,128)S(1)}, f32[4,1024]{1,0:T(4,128)S(1)}) fusion(f32[4,1020,1024]{2,1,0:T(8,128)S(1)} %get-tuple-element.24, f32[1020]{0:T(1024)S(1)} %get-tuple-element.25, f32[4,1024]{1,0:T(4,128)S(1)} %get-tuple-element.23, f32[1020]{0:T(1024)S(1)} %get-tuple-element.26), kind=kLoop, calls=%fused_computation.6 | loop fusion | flops 29233152 | bytes 16785376 | tf_op jit(solution)/shard_map/reduce_sum | solution.py:68
  50.0 3.2 %all-to-all-start.4 = ((s32[4,4,8]{2,1,0:T(4,128)}), s32[4,4,8]{2,1,0:T(4,128)S(1)}, u32[]{:S(2)}, u32[]{:S(2)}) async-start(s32[4,4,8]{2,1,0:T(4,128)} %copy.60), calls=%async_computation.4 | async-start | bytes 16384 | tf_op jit(solution)/shard_map/all_to_all | solution.py:92
  53.4 0.7 reshape.229
  54.2 2.8 %all-to-all-done.4 = s32[4,4,8]{2,1,0:T(4,128)S(1)} async-done(((s32[4,4,8]{2,1,0:T(4,128)}), s32[4,4,8]{2,1,0:T(4,128)S(1)}, u32[]{:S(2)}, u32[]{:S(2)}) %all-to-all-start.4) | async-done | bytes 544 | tf_op jit(solution)/shard_map/all_to_all | solution.py:92
  57.0 5.4 %all-to-all-start = ((f32[8,1,512]{2,1,0:T(1,128)}), f32[8,1,512]{2,1,0:T(1,128)S(1)}, u32[]{:S(2)}, u32[]{:S(2)}) async-start(f32[8,1,512]{2,1,0:T(1,128)} %reshape.229), calls=%async_computation | async-start | bytes 32768 | tf_op jit(solution)/shard_map/all_to_all | solution.py:76
  62.6 0.7 reshape.231
  63.4 5.6 %all-to-all-done = f32[8,1,512]{2,1,0:T(1,128)S(1)} async-done(((f32[8,1,512]{2,1,0:T(1,128)}), f32[8,1,512]{2,1,0:T(1,128)S(1)}, u32[]{:S(2)}, u32[]{:S(2)}) %all-to-all-start) | async-done | bytes 16416 | tf_op jit(solution)/shard_map/all_to_all | solution.py:76
  69.0 3.3 %all-to-all-start.1 = ((f32[8,1,512]{2,1,0:T(1,128)}), f32[8,1,512]{2,1,0:T(1,128)S(1)}, u32[]{:S(2)}, u32[]{:S(2)}) async-start(f32[8,1,512]{2,1,0:T(1,128)} %reshape.231), calls=%async_computation.1 | async-start | bytes 32768 | tf_op jit(solution)/shard_map/all_to_all | solution.py:74
  72.5 0.7 reshape.233
  73.3 5.6 %all-to-all-done.1 = f32[8,1,512]{2,1,0:T(1,128)S(1)} async-done(((f32[8,1,512]{2,1,0:T(1,128)}), f32[8,1,512]{2,1,0:T(1,128)S(1)}, u32[]{:S(2)}, u32[]{:S(2)}) %all-to-all-start.1) | async-done | bytes 16416 | tf_op jit(solution)/shard_map/all_to_all | solution.py:74
  78.8 3.3 %all-to-all-start.2 = ((f32[8,1,512]{2,1,0:T(1,128)}), f32[8,1,512]{2,1,0:T(1,128)S(1)}, u32[]{:S(2)}, u32[]{:S(2)}) async-start(f32[8,1,512]{2,1,0:T(1,128)} %reshape.233), calls=%async_computation.2 | async-start | bytes 32768 | tf_op jit(solution)/shard_map/all_to_all | solution.py:75
  82.4 0.7 reshape.235
  83.5 4.5 %gather_fusion = bf16[128,64,128]{2,1,0:T(8,128)(2,1)} fusion(bf16[4,64,64,128]{3,2,1,0:T(8,128)(2,1)} %param.10, s32[128]{0:T(128)S(1)} %reshape.216), kind=kCustom, calls=%fused_computation | custom fusion | bytes 4195328 | tf_op jit(solution)/shard_map/gather | solution.py:87
  88.7 5.3 %all-to-all-start.3 = ((f32[8,1,512]{2,1,0:T(1,128)}), f32[8,1,512]{2,1,0:T(1,128)S(1)}, u32[]{:S(2)}, u32[]{:S(2)}) async-start(f32[8,1,512]{2,1,0:T(1,128)} %reshape.235), calls=%async_computation.3 | async-start | bytes 32768 | tf_op jit(solution)/shard_map/all_to_all | solution.py:77
  94.0 6.6 %all-to-all-done.3 = f32[8,1,512]{2,1,0:T(1,128)S(1)} async-done(((f32[8,1,512]{2,1,0:T(1,128)}), f32[8,1,512]{2,1,0:T(1,128)S(1)}, u32[]{:S(2)}, u32[]{:S(2)}) %all-to-all-start.3) | async-done | bytes 16416 | tf_op jit(solution)/shard_map/all_to_all | solution.py:77
  100.5 3.6 %all-to-all-start.5 = ((bf16[4,4,8,64,128]{4,3,2,1,0:T(8,128)(2,1)}), bf16[4,4,8,64,128]{4,3,2,1,0:T(8,128)(2,1)S(1)}, u32[]{:S(2)}, u32[]{:S(2)}) async-start(bf16[4,4,8,64,128]{4,3,2,1,0:T(8,128)(2,1)} %bitcast.25), calls=%async_computation.5 | async-start | bytes 4194304 | tf_op jit(solution)/shard_map/all_to_all | solution.py:90
  106.1 0.7 reduce.2
  109.7 20.1 %all-to-all-done.5 = bf16[4,4,8,64,128]{4,3,2,1,0:T(8,128)(2,1)S(1)} async-done(((bf16[4,4,8,64,128]{4,3,2,1,0:T(8,128)(2,1)}), bf16[4,4,8,64,128]{4,3,2,1,0:T(8,128)(2,1)S(1)}, u32[]{:S(2)}, u32[]{:S(2)}) %all-to-all-start.5) | async-done | bytes 2097184 | tf_op jit(solution)/shard_map/all_to_all | solution.py:90
  129.8 0.8 multiply_reduce_fusion.6
  (63 shorter events, 8.0 us)
Async XLA Ops:
  0.6 129.2 %copy-start = (bf16[2,128]{1,0:T(2,128)(2,1)S(1)}, bf16[2,128]{1,0:T(2,128)(2,1)}, u32[]{:S(2)}) copy-start(bf16[2,128]{1,0:T(2,128)(2,1)} %param.9) | copy-start | bytes 1540
  1.9 48.1 %all-to-all-start.6 = ((s32[4,4,8]{2,1,0:T(4,128)}), s32[4,4,8]{2,1,0:T(4,128)S(1)}, u32[]{:S(2)}, u32[]{:S(2)}) async-start(s32[4,4,8]{2,1,0:T(4,128)} %copy.64), calls=%async_computation.6 | async-start | bytes 16384 | tf_op jit(solution)/shard_map/all_to_all | solution.py:91
  43.5 5.9 %copy-start.1 = (s32[4,1,4,8]{3,2,1,0:T(4,128)S(1)}, s32[4,1,4,8]{3,2,1,0:T(4,128)}, u32[]{:S(2)}) copy-start(s32[4,1,4,8]{3,2,1,0:T(4,128)} %param.13) | copy-start | bytes 1540
  43.5 10.7 %copy-start.2 = (s32[2,16,2]{1,2,0:T(2,128)S(1)}, s32[2,16,2]{1,2,0:T(2,128)}, u32[]{:S(2)}) copy-start(s32[2,16,2]{1,2,0:T(2,128)} %param.11) | copy-start | bytes 772
  50.0 7.0 %all-to-all-start.4 = ((s32[4,4,8]{2,1,0:T(4,128)}), s32[4,4,8]{2,1,0:T(4,128)S(1)}, u32[]{:S(2)}, u32[]{:S(2)}) async-start(s32[4,4,8]{2,1,0:T(4,128)} %copy.60), calls=%async_computation.4 | async-start | bytes 16384 | tf_op jit(solution)/shard_map/all_to_all | solution.py:92
  57.0 11.9 %all-to-all-start = ((f32[8,1,512]{2,1,0:T(1,128)}), f32[8,1,512]{2,1,0:T(1,128)S(1)}, u32[]{:S(2)}, u32[]{:S(2)}) async-start(f32[8,1,512]{2,1,0:T(1,128)} %reshape.229), calls=%async_computation | async-start | bytes 32768 | tf_op jit(solution)/shard_map/all_to_all | solution.py:76
  69.0 9.8 %all-to-all-start.1 = ((f32[8,1,512]{2,1,0:T(1,128)}), f32[8,1,512]{2,1,0:T(1,128)S(1)}, u32[]{:S(2)}, u32[]{:S(2)}) async-start(f32[8,1,512]{2,1,0:T(1,128)} %reshape.231), calls=%async_computation.1 | async-start | bytes 32768 | tf_op jit(solution)/shard_map/all_to_all | solution.py:74
  78.8 9.9 %all-to-all-start.2 = ((f32[8,1,512]{2,1,0:T(1,128)}), f32[8,1,512]{2,1,0:T(1,128)S(1)}, u32[]{:S(2)}, u32[]{:S(2)}) async-start(f32[8,1,512]{2,1,0:T(1,128)} %reshape.233), calls=%async_computation.2 | async-start | bytes 32768 | tf_op jit(solution)/shard_map/all_to_all | solution.py:75
  88.7 11.9 %all-to-all-start.3 = ((f32[8,1,512]{2,1,0:T(1,128)}), f32[8,1,512]{2,1,0:T(1,128)S(1)}, u32[]{:S(2)}, u32[]{:S(2)}) async-start(f32[8,1,512]{2,1,0:T(1,128)} %reshape.235), calls=%async_computation.3 | async-start | bytes 32768 | tf_op jit(solution)/shard_map/all_to_all | solution.py:77
  100.5 29.2 %all-to-all-start.5 = ((bf16[4,4,8,64,128]{4,3,2,1,0:T(8,128)(2,1)}), bf16[4,4,8,64,128]{4,3,2,1,0:T(8,128)(2,1)S(1)}, u32[]{:S(2)}, u32[]{:S(2)}) async-start(bf16[4,4,8,64,128]{4,3,2,1,0:T(8,128)(2,1)} %bitcast.25), calls=%async_computation.5 | async-start | bytes 4194304 | tf_op jit(solution)/shard_map/all_to_all | solution.py:90
where the time goes:
time: 132 us; the launch traced here: 131 us
  waiting for transfers between devices  41.3 us (31%)
  blocking collectives  32.6 us (25%)
  starting transfers between devices  28.4 us (22%)
  local copies, waits for them, and re-layouts  12.4 us (9%)
  other arithmetic  10.9 us (8%)
  matrix products  4.82 us (4%)
    all_gather x1, blocking collectives, body(): shard_piece = lax.all_gather(coarse_query, 'blk', axis=0, tiled=True)  32.6 us
    all_to_all x1, waiting for transfers between devices, body(): lax.all_to_all(picked, 'frames', split_axis=0, concat_axis=0, tiled=True)  20.1 us
    all_to_all x1, waiting for transfers between devices, body(): lax.all_to_all(stats[3][None], 'blk', split_axis=2, concat_axis=0, tiled=...  6.56 us
    reduce_sum x1, other arithmetic, body(): row_sums = jnp.sum(weights * local_row[None, None, :], axis=2)  5.89 us
    all_to_all x1, waiting for transfers between devices, body(): lax.all_to_all(stats[2][None], 'blk', split_axis=2, concat_axis=0, tiled=...  5.63 us
    all_to_all x1, waiting for transfers between devices, body(): lax.all_to_all(stats[0][None], 'blk', split_axis=2, concat_axis=0, tiled=...  5.56 us
    all_to_all x1, starting transfers between devices, body(): lax.all_to_all(stats[2][None], 'blk', split_axis=2, concat_axis=0, tiled=...  5.37 us
    all_to_all x1, starting transfers between devices, body(): lax.all_to_all(stats[3][None], 'blk', split_axis=2, concat_axis=0, tiled=...  5.29 us
  transfers between devices with their start and end apart: 7, of which 6 were waited for; matrix products, arithmetic and copies ran while one was open for 19% of the time, Pallas kernels for 0%

commit v1 on v0

--- a/solution.py
+++ b/solution.py
@@ -53,7 +53,12 @@
     local_row = (local_cells // GW).astype(jnp.float32)
     local_col = (local_cells % GW).astype(jnp.float32)
     track_step = max(1, 2048 // heads)
-    shard_piece = lax.all_gather(coarse_query, "blk", axis=0, tiled=True)
+    ring = [coarse_query]
+    for hop in range(7):
+        ring.append(lax.ppermute(ring[-1], "blk", [(dev, (dev + 1) % 8) for dev in range(8)]))
+    shard_piece = jnp.roll(
+        jnp.concatenate(ring[::-1], axis=0), (lax.axis_index("blk") + 1) * ring[0].shape[0], axis=0
+    )
     length = shard_piece.shape[0]
     blocks = []
     for offset in range(0, length, track_step):

time: 132 us -> 150 us (1.14)
  waiting for transfers between devices: 41.3 us -> 78.5 us
  blocking collectives: 32.6 us -> 0 us
  matrix products: 4.82 us -> 10.5 us
  other arithmetic: 10.9 us -> 14.5 us
  local copies, waits for them, and re-layouts: 12.4 us -> 14.9 us
    ppermute x0 -> x7, waiting for transfers between devices: none -> 40 us  [body(): lax.ppermute(ring[-1], 'blk', [(dev, (dev + 1) % 8) for dev in range(8)])]
    all_gather x1 -> x0, blocking collectives: 32.6 us -> none  [body(): shard_piece = lax.all_gather(coarse_query, 'blk', axis=0, tiled=True)]
    dot_general x1, matrix products: 3.99 us -> 8.1 us  [body(): jnp.einsum('rc,fpc->frp', query_rows, coarse_feat, preferred_element_type...]
    ppermute x0 -> x7, starting transfers between devices: none -> 3.06 us  [body(): lax.ppermute(ring[-1], 'blk', [(dev, (dev + 1) % 8) for dev in range(8)])]
    reduce_sum x1, other arithmetic: 5.89 us -> 8.8 us  [body(): row_sums = jnp.sum(weights * local_row[None, None, :], axis=2)]
    all_to_all x1, waiting for transfers between devices: 2.83 us -> 0.01 us  [body(): lax.all_to_all(list_live, 'frames', split_axis=0, concat_axis=0, tiled=True)]
    all_to_all x1, starting transfers between devices: 5.37 us -> 3.34 us  [body(): lax.all_to_all(stats[2][None], 'blk', split_axis=2, concat_axis=0, tiled=...]
    sub x1, matrix products: 0.83 us -> 2.43 us  [refine_frame(): weights = jnp.exp(scores - highest)]
  transfers between devices with their start and end apart: 7 -> 14, of which waited for: 6 -> 12; matrix products, arithmetic and copies ran while one was open for 19% -> 25% of each run, Pallas kernels for 0% -> 0%
where the time goes in v1:
time: 150 us; the launch traced here: 149 us
  waiting for transfers between devices  78.5 us (52%)
  starting transfers between devices  29.3 us (20%)
  local copies, waits for them, and re-layouts  14.9 us (10%)
  other arithmetic  14.5 us (10%)
  matrix products  10.5 us (7%)
    ppermute x7, waiting for transfers between devices, body(): lax.ppermute(ring[-1], 'blk', [(dev, (dev + 1) % 8) for dev in range(8)])  40 us
    all_to_all x1, waiting for transfers between devices, body(): lax.all_to_all(picked, 'frames', split_axis=0, concat_axis=0, tiled=True)  20.2 us
    reduce_sum x1, other arithmetic, body(): row_sums = jnp.sum(weights * local_row[None, None, :], axis=2)  8.8 us
    dot_general x1, matrix products, body(): jnp.einsum('rc,fpc->frp', query_rows, coarse_feat, preferred_element_type...  8.1 us
    all_to_all x1, waiting for transfers between devices, body(): lax.all_to_all(stats[3][None], 'blk', split_axis=2, concat_axis=0, tiled=...  6.56 us
    all_to_all x1, waiting for transfers between devices, body(): lax.all_to_all(stats[0][None], 'blk', split_axis=2, concat_axis=0, tiled=...  5.56 us
    all_to_all x1, waiting for transfers between devices, body(): lax.all_to_all(stats[2][None], 'blk', split_axis=2, concat_axis=0, tiled=...  5.56 us
    all_to_all x1, starting transfers between devices, body(): lax.all_to_all(stats[3][None], 'blk', split_axis=2, concat_axis=0, tiled=...  5.29 us
  transfers between devices with their start and end apart: 14, of which 12 were waited for; matrix products, arithmetic and copies ran while one was open for 25% of the time, Pallas kernels for 0%

profile of v1, /device:TPU:0, one launch (start us, length us, event | category | flops | bytes accessed | tf_op | source)
XLA Modules:
  0.0 148.8 jit_solution(3827617597048447517)
XLA Ops:
  0.6 3.0 %collective-permute-start = (bf16[8,16,256]{2,1,0:T(8,128)(2,1)}, bf16[8,16,256]{2,1,0:T(8,128)(2,1)S(1)}, u32[]{:S(2)}, u32[]{:S(2)}) collective-permute-start(bf16[8,16,256]{2,1,0:T(8,128)(2,1)} %param.7), channel_id=1, source_target_pairs={{0,4},{4,8},{8,12},{12,16},{16,20},{20,24},{24,28},{28,0},{1,5},{5... | collective-permute-start | bytes 196616 | tf_op jit(solution)/shard_map/ppermute | solution.py:58
  3.7 5.5 %collective-permute-done = bf16[8,16,256]{2,1,0:T(8,128)(2,1)S(1)} collective-permute-done((bf16[8,16,256]{2,1,0:T(8,128)(2,1)}, bf16[8,16,256]{2,1,0:T(8,128)(2,1)S(1)}, u32[]{:S(2)}, u32[]{:S(2)}) %collective-permute-start) | collective-permute-done | bytes 65568 | tf_op jit(solution)/shard_map/ppermute | solution.py:58
  9.2 7.0 %collective-permute-done.1 = bf16[8,16,256]{2,1,0:T(8,128)(2,1)S(1)} collective-permute-done((bf16[8,16,256]{2,1,0:T(8,128)(2,1)S(1)}, bf16[8,16,256]{2,1,0:T(8,128)(2,1)S(1)}, u32[]{:S(2)}, u32[]{:S(2)}) %collective-permute-start.1) | collective-permute-done | bytes 65568 | tf_op jit(solution)/shard_map/ppermute | solution.py:58
  16.2 7.0 %collective-permute-done.2 = bf16[8,16,256]{2,1,0:T(8,128)(2,1)S(1)} collective-permute-done((bf16[8,16,256]{2,1,0:T(8,128)(2,1)S(1)}, bf16[8,16,256]{2,1,0:T(8,128)(2,1)S(1)}, u32[]{:S(2)}, u32[]{:S(2)}) %collective-permute-start.2) | collective-permute-done | bytes 65568 | tf_op jit(solution)/shard_map/ppermute | solution.py:58
  23.1 1.3 copy.64
  24.4 3.2 %all-to-all-start.6 = ((s32[4,4,8]{2,1,0:T(4,128)}), s32[4,4,8]{2,1,0:T(4,128)S(1)}, u32[]{:S(2)}, u32[]{:S(2)}) async-start(s32[4,4,8]{2,1,0:T(4,128)} %copy.64), calls=%async_computation.6 | async-start | bytes 16384 | tf_op jit(solution)/shard_map/all_to_all | solution.py:96
  27.7 2.4 %collective-permute-done.3 = bf16[8,16,256]{2,1,0:T(8,128)(2,1)S(1)} collective-permute-done((bf16[8,16,256]{2,1,0:T(8,128)(2,1)S(1)}, bf16[8,16,256]{2,1,0:T(8,128)(2,1)S(1)}, u32[]{:S(2)}, u32[]{:S(2)}) %collective-permute-start.3) | collective-permute-done | bytes 65568 | tf_op jit(solution)/shard_map/ppermute | solution.py:58
  30.8 6.3 %collective-permute-done.4 = bf16[8,16,256]{2,1,0:T(8,128)(2,1)S(1)} collective-permute-done((bf16[8,16,256]{2,1,0:T(8,128)(2,1)S(1)}, bf16[8,16,256]{2,1,0:T(8,128)(2,1)S(1)}, u32[]{:S(2)}, u32[]{:S(2)}) %collective-permute-start.4) | collective-permute-done | bytes 65568 | tf_op jit(solution)/shard_map/ppermute | solution.py:58
  39.0 5.0 %collective-permute-done.5 = bf16[8,16,256]{2,1,0:T(8,128)(2,1)S(1)} collective-permute-done((bf16[8,16,256]{2,1,0:T(8,128)(2,1)S(1)}, bf16[8,16,256]{2,1,0:T(8,128)(2,1)S(1)}, u32[]{:S(2)}, u32[]{:S(2)}) %collective-permute-start.5) | collective-permute-done | bytes 65568 | tf_op jit(solution)/shard_map/ppermute | solution.py:58
  44.0 6.9 %collective-permute-done.6 = bf16[8,16,256]{2,1,0:T(8,128)(2,1)S(1)} collective-permute-done((bf16[8,16,256]{2,1,0:T(8,128)(2,1)S(1)}, bf16[8,16,256]{2,1,0:T(8,128)(2,1)S(1)}, u32[]{:S(2)}, u32[]{:S(2)}) %collective-permute-start.6) | collective-permute-done | bytes 65568 | tf_op jit(solution)/shard_map/ppermute | solution.py:58
  52.9 8.1 %bitcast_reduce_fusion = (f32[4,1024]{1,0:T(4,128)S(1)}, f32[1024,4,1020]{0,2,1:T(8,128)}) fusion(bf16[1024,256,1]{1,0,2:T(8,128)(2,1)S(1)} %bitcast.97, bf16[4,1020,256]{2,0,1:T(4,128)(2,1)S(1)} %copy-done), kind=kOutput, calls=%fused_computation.3 | convolution fusion | flops 2147446784 | bytes 19341312 | tf_op jit(solution)/shard_map/rc,fpc->frp/dot_general | solution.py:67
  61.0 3.2 %all-to-all-start.4 = ((s32[4,4,8]{2,1,0:T(4,128)}), s32[4,4,8]{2,1,0:T(4,128)S(1)}, u32[]{:S(2)}, u32[]{:S(2)}) async-start(s32[4,4,8]{2,1,0:T(4,128)} %copy.60), calls=%async_computation.4 | async-start | bytes 16384 | tf_op jit(solution)/shard_map/all_to_all | solution.py:97
  64.2 8.8 %multiply_reduce_fusion.1 = (f32[4,1024]{1,0:T(4,128)S(1)}, f32[4,1024]{1,0:T(4,128)S(1)}, f32[4,1024]{1,0:T(4,128)S(1)}) fusion(f32[1024,4,1020]{0,2,1:T(8,128)} %get-tuple-element.24, f32[1020]{0:T(1024)S(1)} %get-tuple-element.25, f32[4,1024]{1,0:T(4,128)S(1)} %get-tuple-element.23, f32[1020]{0:T(1024)S(1)} %get-tuple-element.26), kind=kLoop, calls=%fused_computation.6 | loop fusion | flops 29233152 | bytes 16785376 | tf_op jit(solution)/shard_map/reduce_sum | solution.py:73
  74.0 3.3 %all-to-all-start = ((f32[8,1,512]{2,1,0:T(1,128)}), f32[8,1,512]{2,1,0:T(1,128)S(1)}, u32[]{:S(2)}, u32[]{:S(2)}) async-start(f32[8,1,512]{2,1,0:T(1,128)} %reshape.229), calls=%async_computation | async-start | bytes 32768 | tf_op jit(solution)/shard_map/all_to_all | solution.py:81
  78.3 5.6 %all-to-all-done = f32[8,1,512]{2,1,0:T(1,128)S(1)} async-done(((f32[8,1,512]{2,1,0:T(1,128)}), f32[8,1,512]{2,1,0:T(1,128)S(1)}, u32[]{:S(2)}, u32[]{:S(2)}) %all-to-all-start) | async-done | bytes 16416 | tf_op jit(solution)/shard_map/all_to_all | solution.py:81
  83.9 3.3 %all-to-all-start.1 = ((f32[8,1,512]{2,1,0:T(1,128)}), f32[8,1,512]{2,1,0:T(1,128)S(1)}, u32[]{:S(2)}, u32[]{:S(2)}) async-start(f32[8,1,512]{2,1,0:T(1,128)} %reshape.231), calls=%async_computation.1 | async-start | bytes 32768 | tf_op jit(solution)/shard_map/all_to_all | solution.py:79
  88.1 5.6 %all-to-all-done.1 = f32[8,1,512]{2,1,0:T(1,128)S(1)} async-done(((f32[8,1,512]{2,1,0:T(1,128)}), f32[8,1,512]{2,1,0:T(1,128)S(1)}, u32[]{:S(2)}, u32[]{:S(2)}) %all-to-all-start.1) | async-done | bytes 16416 | tf_op jit(solution)/shard_map/all_to_all | solution.py:79
  93.7 3.3 %all-to-all-start.2 = ((f32[8,1,512]{2,1,0:T(1,128)}), f32[8,1,512]{2,1,0:T(1,128)S(1)}, u32[]{:S(2)}, u32[]{:S(2)}) async-start(f32[8,1,512]{2,1,0:T(1,128)} %reshape.233), calls=%async_computation.2 | async-start | bytes 32768 | tf_op jit(solution)/shard_map/all_to_all | solution.py:80
  97.5 4.5 %gather_fusion = bf16[128,64,128]{2,1,0:T(8,128)(2,1)} fusion(bf16[4,64,64,128]{3,2,1,0:T(8,128)(2,1)} %param.10, s32[128]{0:T(128)S(1)} %reshape.216), kind=kCustom, calls=%fused_computation | custom fusion | bytes 4195328 | tf_op jit(solution)/shard_map/gather | solution.py:92
  103.6 5.3 %all-to-all-start.3 = ((f32[8,1,512]{2,1,0:T(1,128)}), f32[8,1,512]{2,1,0:T(1,128)S(1)}, u32[]{:S(2)}, u32[]{:S(2)}) async-start(f32[8,1,512]{2,1,0:T(1,128)} %reshape.235), calls=%async_computation.3 | async-start | bytes 32768 | tf_op jit(solution)/shard_map/all_to_all | solution.py:82
  108.9 6.6 %all-to-all-done.3 = f32[8,1,512]{2,1,0:T(1,128)S(1)} async-done(((f32[8,1,512]{2,1,0:T(1,128)}), f32[8,1,512]{2,1,0:T(1,128)S(1)}, u32[]{:S(2)}, u32[]{:S(2)}) %all-to-all-start.3) | async-done | bytes 16416 | tf_op jit(solution)/shard_map/all_to_all | solution.py:82
  115.4 4.4 %all-to-all-start.5 = ((bf16[4,4,8,64,128]{4,3,2,1,0:T(8,128)(2,1)}), bf16[4,4,8,64,128]{4,3,2,1,0:T(8,128)(2,1)}, u32[]{:S(2)}, u32[]{:S(2)}) async-start(bf16[4,4,8,64,128]{4,3,2,1,0:T(8,128)(2,1)} %bitcast.96), calls=%async_computation.5 | async-start | bytes 4194304 | tf_op jit(solution)/shard_map/all_to_all | solution.py:95
  125.4 20.2 %all-to-all-done.5 = bf16[4,4,8,64,128]{4,3,2,1,0:T(8,128)(2,1)} async-done(((bf16[4,4,8,64,128]{4,3,2,1,0:T(8,128)(2,1)}), bf16[4,4,8,64,128]{4,3,2,1,0:T(8,128)(2,1)}, u32[]{:S(2)}, u32[]{:S(2)}) %all-to-all-start.5) | async-done | bytes 2097184 | tf_op jit(solution)/shard_map/all_to_all | solution.py:95
  145.6 2.4 %multiply_reduce_fusion.6 = (f32[16,2]{1,0:T(8,128)S(1)}, f32[16,2]{1,0:T(8,128)S(1)}, f32[16,2]{1,0:T(8,128)S(1)}) fusion(f32[16,512]{1,0:T(8,128)S(1)} %get-tuple-element.28, f32[16,512]{1,0:T(8,128)S(1)} %get-tuple-element.27, bf16[16,512,128]{2,1,0:T(8,128)(2,1)} %bitcast.26, pred[16,512]{1,0:T(8,128)(4,1)S(1)} %broadcast_in_dim.17, ...), kind=kOutput, calls=%fused_computation.21 | convolution fusion | flops 4440511 | bytes 2172032 | tf_op jit(solution)/shard_map/vmap()/sub | solution.py:32
  (91 shorter events, 15.5 us)
Async XLA Ops:
  0.6 52.3 %copy-start = (bf16[4,1020,256]{2,0,1:T(4,128)(2,1)S(1)}, bf16[4,1020,256]{2,0,1:T(4,128)(2,1)}, u32[]{:S(2)}) copy-start(bf16[4,1020,256]{2,0,1:T(4,128)(2,1)} %param.8) | copy-start | bytes 6266884
  0.6 8.5 %collective-permute-start = (bf16[8,16,256]{2,1,0:T(8,128)(2,1)}, bf16[8,16,256]{2,1,0:T(8,128)(2,1)S(1)}, u32[]{:S(2)}, u32[]{:S(2)}) collective-permute-start(bf16[8,16,256]{2,1,0:T(8,128)(2,1)} %param.7), channel_id=1, source_target_pairs={{0,4},{4,8},{8,12},{12,16},{16,20},{20,24},{24,28},{28,0},{1,5},{5... | collective-permute-start | bytes 196616 | tf_op jit(solution)/shard_map/ppermute | solution.py:58
  9.2 7.0 %collective-permute-start.1 = (bf16[8,16,256]{2,1,0:T(8,128)(2,1)S(1)}, bf16[8,16,256]{2,1,0:T(8,128)(2,1)S(1)}, u32[]{:S(2)}, u32[]{:S(2)}) collective-permute-start(bf16[8,16,256]{2,1,0:T(8,128)(2,1)S(1)} %collective-permute-done), channel_id=1, source_target_pairs={{0,4},{4,8},{8,12},{12,16},{16,20},{20,24},{24,28},{28,0},{1,5},{5... | collective-permute-start | bytes 196616 | tf_op jit(solution)/shard_map/ppermute | solution.py:58
  16.2 7.0 %collective-permute-start.2 = (bf16[8,16,256]{2,1,0:T(8,128)(2,1)S(1)}, bf16[8,16,256]{2,1,0:T(8,128)(2,1)S(1)}, u32[]{:S(2)}, u32[]{:S(2)}) collective-permute-start(bf16[8,16,256]{2,1,0:T(8,128)(2,1)S(1)} %collective-permute-done.1), channel_id=1, source_target_pairs={{0,4},{4,8},{8,12},{12,16},{16,20},{20,24},{24,28},{28,0},{1,5},{5... | collective-permute-start | bytes 196616 | tf_op jit(solution)/shard_map/ppermute | solution.py:58
  23.1 7.0 %collective-permute-start.3 = (bf16[8,16,256]{2,1,0:T(8,128)(2,1)S(1)}, bf16[8,16,256]{2,1,0:T(8,128)(2,1)S(1)}, u32[]{:S(2)}, u32[]{:S(2)}) collective-permute-start(bf16[8,16,256]{2,1,0:T(8,128)(2,1)S(1)} %collective-permute-done.2), channel_id=1, source_target_pairs={{0,4},{4,8},{8,12},{12,16},{16,20},{20,24},{24,28},{28,0},{1,5},{5... | collective-permute-start | bytes 196616 | tf_op jit(solution)/shard_map/ppermute | solution.py:58
  24.4 36.6 %all-to-all-start.6 = ((s32[4,4,8]{2,1,0:T(4,128)}), s32[4,4,8]{2,1,0:T(4,128)S(1)}, u32[]{:S(2)}, u32[]{:S(2)}) async-start(s32[4,4,8]{2,1,0:T(4,128)} %copy.64), calls=%async_computation.6 | async-start | bytes 16384 | tf_op jit(solution)/shard_map/all_to_all | solution.py:96
  30.1 7.0 %collective-permute-start.4 = (bf16[8,16,256]{2,1,0:T(8,128)(2,1)S(1)}, bf16[8,16,256]{2,1,0:T(8,128)(2,1)S(1)}, u32[]{:S(2)}, u32[]{:S(2)}) collective-permute-start(bf16[8,16,256]{2,1,0:T(8,128)(2,1)S(1)} %collective-permute-done.3), channel_id=1, source_target_pairs={{0,4},{4,8},{8,12},{12,16},{16,20},{20,24},{24,28},{28,0},{1,5},{5... | collective-permute-start | bytes 196616 | tf_op jit(solution)/shard_map/ppermute | solution.py:58
  37.0 7.0 %collective-permute-start.5 = (bf16[8,16,256]{2,1,0:T(8,128)(2,1)S(1)}, bf16[8,16,256]{2,1,0:T(8,128)(2,1)S(1)}, u32[]{:S(2)}, u32[]{:S(2)}) collective-permute-start(bf16[8,16,256]{2,1,0:T(8,128)(2,1)S(1)} %collective-permute-done.4), channel_id=1, source_target_pairs={{0,4},{4,8},{8,12},{12,16},{16,20},{20,24},{24,28},{28,0},{1,5},{5... | collective-permute-start | bytes 196616 | tf_op jit(solution)/shard_map/ppermute | solution.py:58
  44.0 7.0 %collective-permute-start.6 = (bf16[8,16,256]{2,1,0:T(8,128)(2,1)S(1)}, bf16[8,16,256]{2,1,0:T(8,128)(2,1)S(1)}, u32[]{:S(2)}, u32[]{:S(2)}) collective-permute-start(bf16[8,16,256]{2,1,0:T(8,128)(2,1)S(1)} %collective-permute-done.5), channel_id=1, source_target_pairs={{0,4},{4,8},{8,12},{12,16},{16,20},{20,24},{24,28},{28,0},{1,5},{5... | collective-permute-start | bytes 196616 | tf_op jit(solution)/shard_map/ppermute | solution.py:58
  61.0 13.0 %all-to-all-start.4 = ((s32[4,4,8]{2,1,0:T(4,128)}), s32[4,4,8]{2,1,0:T(4,128)S(1)}, u32[]{:S(2)}, u32[]{:S(2)}) async-start(s32[4,4,8]{2,1,0:T(4,128)} %copy.60), calls=%async_computation.4 | async-start | bytes 16384 | tf_op jit(solution)/shard_map/all_to_all | solution.py:97
  74.0 9.9 %all-to-all-start = ((f32[8,1,512]{2,1,0:T(1,128)}), f32[8,1,512]{2,1,0:T(1,128)S(1)}, u32[]{:S(2)}, u32[]{:S(2)}) async-start(f32[8,1,512]{2,1,0:T(1,128)} %reshape.229), calls=%async_computation | async-start | bytes 32768 | tf_op jit(solution)/shard_map/all_to_all | solution.py:81
  83.9 9.8 %all-to-all-start.1 = ((f32[8,1,512]{2,1,0:T(1,128)}), f32[8,1,512]{2,1,0:T(1,128)S(1)}, u32[]{:S(2)}, u32[]{:S(2)}) async-start(f32[8,1,512]{2,1,0:T(1,128)} %reshape.231), calls=%async_computation.1 | async-start | bytes 32768 | tf_op jit(solution)/shard_map/all_to_all | solution.py:79
  93.7 9.9 %all-to-all-start.2 = ((f32[8,1,512]{2,1,0:T(1,128)}), f32[8,1,512]{2,1,0:T(1,128)S(1)}, u32[]{:S(2)}, u32[]{:S(2)}) async-start(f32[8,1,512]{2,1,0:T(1,128)} %reshape.233), calls=%async_computation.2 | async-start | bytes 32768 | tf_op jit(solution)/shard_map/all_to_all | solution.py:80
  102.0 43.6 %copy-start.1 = (bf16[2,128]{1,0:T(2,128)(2,1)S(1)}, bf16[2,128]{1,0:T(2,128)(2,1)}, u32[]{:S(2)}) copy-start(bf16[2,128]{1,0:T(2,128)(2,1)} %param.9) | copy-start | bytes 1540
  103.6 11.9 %all-to-all-start.3 = ((f32[8,1,512]{2,1,0:T(1,128)}), f32[8,1,512]{2,1,0:T(1,128)S(1)}, u32[]{:S(2)}, u32[]{:S(2)}) async-start(f32[8,1,512]{2,1,0:T(1,128)} %reshape.235), calls=%async_computation.3 | async-start | bytes 32768 | tf_op jit(solution)/shard_map/all_to_all | solution.py:82
  115.4 30.2 %all-to-all-start.5 = ((bf16[4,4,8,64,128]{4,3,2,1,0:T(8,128)(2,1)}), bf16[4,4,8,64,128]{4,3,2,1,0:T(8,128)(2,1)}, u32[]{:S(2)}, u32[]{:S(2)}) async-start(bf16[4,4,8,64,128]{4,3,2,1,0:T(8,128)(2,1)} %bitcast.96), calls=%async_computation.5 | async-start | bytes 4194304 | tf_op jit(solution)/shard_map/all_to_all | solution.py:95
